TPU v7x, 128 devices: a whole 4x4x4 slice. The times are simulated.
128 devices in a mesh: row: 16 (over z_lo, y, core), col: 8 (over x, z_hi).
Axes of the slice: x: 4, y: 4, z: 4 (z_hi: 2, z_lo: 2; z = z_hi * 2 + z_lo), core: 2. Of those that a mesh axis runs over, the one named last changes fastest.
Arguments:
- pair: bfloat16 [1024, 1024, 128], P('row', 'col'), may hold values from -6 to 6
- ln_gain: float32 [128], replicated, may hold values from 0.1 to 1.9
- ln_bias: float32 [128], replicated, may hold values from -3 to 3
- gate_weight: bfloat16 [128, 512], replicated, may hold values from -0.5 to 0.5
- up_weight: bfloat16 [128, 512], replicated, may hold values from -0.5 to 0.5
- out_weight: bfloat16 [512, 128], replicated, may hold values from -0.25 to 0.25
- head_weight: bfloat16 [128, 64], replicated, may hold values from -1 to 1
- targets: int32 [1024, 1024], P(('row', 'col')), may hold values from 0 to 63
- pair_mask: int32 [1024, 1024], P(('row', 'col')), may hold values 0 or 1
Outputs:
- pair_out: bfloat16 [1024, 1024, 128], P('row', 'col')
- loss: float32 [], replicated
- grad_gain: float32 [128], replicated
- grad_bias: float32 [128], replicated
- grad_gate: float32 [128, 512], replicated
- grad_up: float32 [128, 512], replicated
- grad_out: float32 [512, 128], replicated
- grad_head: float32 [128, 64], replicated
All inputs are finite; a program needn't handle non-finite values. No bound on the sum of `pair_mask` on one device may be relied on, other than what follows from the above.
Results may differ from a plain program's by a relative error of at most 0.001.
The roundings to bfloat16 on the way count: a program that leaves them out, or rounds other values in their place, can miss the bound.
Values may be sent and summed in bfloat16 or wider, within the bound.
No kernel may reach another device: no remote copies, remote signals or barrier semaphores. Data moves between devices by JAX's collectives and lax.ppermute only.
A program may use at most 64 MiB of HBM per device.

v0:
```python
import math
import jax
import jax.numpy as jnp
from jax import lax
from jax.sharding import PartitionSpec as P

EPSILON = 1e-05


def normalize(rows_in, ln_gain, ln_bias):
    values = rows_in.astype(jnp.float32)
    centered = values - jnp.mean(values, axis=-1, keepdims=True)
    variance = jnp.mean(centered * centered, axis=-1, keepdims=True)
    unit_rows = centered * lax.rsqrt(variance + EPSILON)
    normed = (unit_rows * ln_gain + ln_bias).astype(jnp.bfloat16)
    return (unit_rows, normed)


def inner(left, right):
    return lax.dot_general(
        left, right, (((0,), (0,)), ((), ())), preferred_element_type=jnp.float32
    )


def advance(rows_in, ln_gain, ln_bias, gate_weight, up_weight, out_weight):
    unit_rows, normed = normalize(rows_in, ln_gain, ln_bias)
    gate_pre = jnp.dot(normed, gate_weight, preferred_element_type=jnp.float32)
    up_pre = jnp.dot(normed, up_weight, preferred_element_type=jnp.float32)
    hidden = (jax.nn.silu(gate_pre) * up_pre).astype(jnp.bfloat16)
    update = jnp.dot(hidden, out_weight, preferred_element_type=jnp.float32)
    return (rows_in.astype(jnp.float32) + update).astype(jnp.bfloat16)


def retreat(totals, rows_in, grad_rows, ln_gain, ln_bias, gate_weight, up_weight, out_weight):
    unit_rows, normed = normalize(rows_in, ln_gain, ln_bias)
    gate_pre = jnp.dot(normed, gate_weight, preferred_element_type=jnp.float32)
    up_pre = jnp.dot(normed, up_weight, preferred_element_type=jnp.float32)
    squashed = jax.nn.sigmoid(gate_pre)
    silu_val = gate_pre * squashed
    hidden = (silu_val * up_pre).astype(jnp.bfloat16)
    grad_hidden = jnp.dot(grad_rows, out_weight.T, preferred_element_type=jnp.float32)
    grad_gate_pre = (grad_hidden * up_pre * squashed * (1.0 + gate_pre * (1.0 - squashed))).astype(
        jnp.bfloat16
    )
    grad_up_pre = (grad_hidden * silu_val).astype(jnp.bfloat16)
    grad_normed = jnp.dot(
        grad_gate_pre, gate_weight.T, preferred_element_type=jnp.float32
    ) + jnp.dot(grad_up_pre, up_weight.T, preferred_element_type=jnp.float32)
    sum_gain, sum_bias, sum_gate, sum_up, sum_out = totals
    return (
        sum_gain + jnp.sum(grad_normed * unit_rows, axis=0),
        sum_bias + jnp.sum(grad_normed, axis=0),
        sum_gate + inner(normed, grad_gate_pre),
        sum_up + inner(normed, grad_up_pre),
        sum_out + inner(hidden, grad_rows),
    )


def loss_terms(logits, targets, pair_mask):
    bins = logits.shape[-1]
    one_hot = (targets[..., None] == jnp.arange(bins, dtype=jnp.int32)).astype(jnp.float32)
    log_total = jnp.log(jnp.sum(jnp.exp(logits), axis=-1))
    weights_mask = pair_mask.astype(jnp.float32)
    loss_part = jnp.sum(weights_mask * (log_total - jnp.sum(logits * one_hot, axis=-1)))
    soft_probs = jnp.exp(logits - log_total[..., None])
    return (loss_part, soft_probs)


def grad_from(soft_probs, targets, pair_mask, tokens):
    bins = soft_probs.shape[-1]
    one_hot = (targets[..., None] == jnp.arange(bins, dtype=jnp.int32)).astype(jnp.float32)
    weights_mask = pair_mask.astype(jnp.float32)
    return (weights_mask[..., None] * (soft_probs - one_hot) / tokens).astype(jnp.bfloat16)


def shards(
    pair, ln_gain, ln_bias, gate_weight, up_weight, out_weight, head_weight, targets, pair_mask
):
    rows_tile, cols_tile, width = pair.shape
    tokens = cols_tile * lax.axis_size("col")
    block_rows = math.gcd(rows_tile, max(1, 2048 // cols_tile))
    count = rows_tile // block_rows
    blocks = pair.reshape(count, block_rows * cols_tile, width)

    def forward_one(rows_in):
        return advance(rows_in, ln_gain, ln_bias, gate_weight, up_weight, out_weight)

    pair_out = lax.map(forward_one, blocks).reshape(pair.shape)
    rows_pair = lax.all_to_all(pair_out, "col", split_axis=0, concat_axis=1, tiled=True)
    flip_pair = lax.all_to_all(
        jnp.swapaxes(rows_pair, 0, 1), ("row", "col"), split_axis=0, concat_axis=1, tiled=True
    )
    half_rows = jnp.dot(rows_pair, head_weight, preferred_element_type=jnp.float32).astype(
        jnp.bfloat16
    )
    half_flip = jnp.dot(flip_pair, head_weight, preferred_element_type=jnp.float32).astype(
        jnp.bfloat16
    )
    logits = half_rows.astype(jnp.float32) + half_flip.astype(jnp.float32)
    loss_part, soft_probs = loss_terms(logits, targets, pair_mask)
    grad_logits = grad_from(soft_probs, targets, pair_mask, tokens)
    grad_flip = lax.all_to_all(
        jnp.swapaxes(grad_logits, 0, 1), ("row", "col"), split_axis=0, concat_axis=1, tiled=True
    )
    tile_grad, tile_flip = (
        lax.all_to_all(grad_logits, "col", split_axis=1, concat_axis=0, tiled=True),
        lax.all_to_all(grad_flip, "col", split_axis=1, concat_axis=0, tiled=True),
    )
    bins = head_weight.shape[1]
    flat_out = pair_out.reshape(-1, width)
    grad_head = inner(flat_out, tile_grad.reshape(-1, bins)) + inner(
        flat_out, tile_flip.reshape(-1, bins)
    )
    head_back = head_weight.T
    grad_pair = (
        jnp.dot(tile_grad, head_back, preferred_element_type=jnp.float32)
        + jnp.dot(tile_flip, head_back, preferred_element_type=jnp.float32)
    ).astype(jnp.bfloat16)
    grad_blocks = grad_pair.reshape(count, block_rows * cols_tile, width)
    hidden_width = gate_weight.shape[1]
    start = (
        jnp.zeros((width,), jnp.float32),
        jnp.zeros((width,), jnp.float32),
        jnp.zeros((width, hidden_width), jnp.float32),
        jnp.zeros((width, hidden_width), jnp.float32),
        jnp.zeros((hidden_width, width), jnp.float32),
    )

    def backward_one(totals, inputs):
        return (
            retreat(
                totals, inputs[0], inputs[1], ln_gain, ln_bias, gate_weight, up_weight, out_weight
            ),
            None,
        )

    totals, unused = lax.scan(backward_one, start, (blocks, grad_blocks))
    summed = lax.psum(
        (loss_part, totals[0], totals[1], totals[2], totals[3], totals[4], grad_head),
        ("row", "col"),
    )
    loss = summed[0] / (tokens * tokens)
    return (pair_out, loss, summed[1], summed[2], summed[3], summed[4], summed[5], summed[6])


def solution(mesh):
    placed = (
        P("row", "col", None),
        P(),
        P(),
        P(),
        P(),
        P(),
        P(),
        P(("row", "col"), None),
        P(("row", "col"), None),
    )
    return jax.shard_map(
        shards,
        mesh=mesh,
        in_specs=placed,
        out_specs=(P("row", "col", None), P(), P(), P(), P(), P(), P(), P()),
        check_vma=False,
    )
```

profile of v0, /device:TPU:1, one launch (start us, length us, event | category | flops | bytes accessed | tf_op | source)
XLA Modules:
  0.0 416.3 jit_solution(17993143803311774811)
XLA Ops:
  7.2 47.0 %while.29 = (s32[]{:T(128)}, bf16[4,2048,128]{2,1,0:T(8,128)(2,1)}, bf16[4,2048,128]{2,1,0:T(8,128)(2,1)}, f32[128]{0:T(128)}, f32[128]{0:T(128)}, /*index=5*/bf...) while((s32[]{:T(128)}, bf16[4,2048,128]{2,1,0:T(8,128)(2,1)}, ...), condition=%wide.region_3.4_spmd, body=%wide.region_0.3_spmd.sunk | while | flops 817104896 | bytes 21462268 | solution.py:88
  7.2 1.3 convert_reduce_fusion.4
  8.5 1.7 fusion.136
  10.2 4.0 fusion.137
  14.2 4.7 %fusion.138 = bf16[4,2048,128]{2,1,0:T(8,128)(2,1)} fusion(bf16[4,2048,128]{2,1,0:T(8,128)(2,1)} %get-tuple-element.382, s32[]{:T(128)S(6)} %copy.70, bf16[512,128]{1,0:T(8,128)(2,1)S(1)} %copy-done.22, f32[2048,512]{1,0:T(8,128)} %fusion.137, bf16[128,512]{1,0:T(8,128)(2,1)S(1)} %copy-done.12, f32[128]{0:T(128)S(1)} %copy-done.17, ...), kind=kOutput, calls=%fused_computation.4.clone.1 | convolution fusion | flops 545521664 | bytes 6047744 | tf_op jit(solution)/shard_map/while/body/eval_jaxpr/dot_general | solution.py:30
  18.9 1.2 convert_reduce_fusion.4
  20.2 1.7 fusion.136
  22.0 4.0 fusion.137
  26.0 4.7 %fusion.138 = bf16[4,2048,128]{2,1,0:T(8,128)(2,1)} fusion(bf16[4,2048,128]{2,1,0:T(8,128)(2,1)} %get-tuple-element.382, s32[]{:T(128)S(6)} %copy.70, bf16[512,128]{1,0:T(8,128)(2,1)S(1)} %copy-done.22, f32[2048,512]{1,0:T(8,128)} %fusion.137, bf16[128,512]{1,0:T(8,128)(2,1)S(1)} %copy-done.12, f32[128]{0:T(128)S(1)} %copy-done.17, ...), kind=kOutput, calls=%fused_computation.4.clone.1 | convolution fusion | flops 545521664 | bytes 6047744 | tf_op jit(solution)/shard_map/while/body/eval_jaxpr/dot_general | solution.py:30
  30.7 1.2 convert_reduce_fusion.4
  31.9 1.7 fusion.136
  33.7 4.0 fusion.137
  37.7 4.7 %fusion.138 = bf16[4,2048,128]{2,1,0:T(8,128)(2,1)} fusion(bf16[4,2048,128]{2,1,0:T(8,128)(2,1)} %get-tuple-element.382, s32[]{:T(128)S(6)} %copy.70, bf16[512,128]{1,0:T(8,128)(2,1)S(1)} %copy-done.22, f32[2048,512]{1,0:T(8,128)} %fusion.137, bf16[128,512]{1,0:T(8,128)(2,1)S(1)} %copy-done.12, f32[128]{0:T(128)S(1)} %copy-done.17, ...), kind=kOutput, calls=%fused_computation.4.clone.1 | convolution fusion | flops 545521664 | bytes 6047744 | tf_op jit(solution)/shard_map/while/body/eval_jaxpr/dot_general | solution.py:30
  42.4 1.2 convert_reduce_fusion.4
  43.7 1.7 fusion.136
  45.4 4.0 fusion.137
  49.4 4.7 %fusion.138 = bf16[4,2048,128]{2,1,0:T(8,128)(2,1)} fusion(bf16[4,2048,128]{2,1,0:T(8,128)(2,1)} %get-tuple-element.382, s32[]{:T(128)S(6)} %copy.70, bf16[512,128]{1,0:T(8,128)(2,1)S(1)} %copy-done.22, f32[2048,512]{1,0:T(8,128)} %fusion.137, bf16[128,512]{1,0:T(8,128)(2,1)S(1)} %copy-done.12, f32[128]{0:T(128)S(1)} %copy-done.17, ...), kind=kOutput, calls=%fused_computation.4.clone.1 | convolution fusion | flops 545521664 | bytes 6047744 | tf_op jit(solution)/shard_map/while/body/eval_jaxpr/dot_general | solution.py:30
  54.2 34.8 %all_to_all.90 = bf16[64,128,128]{2,1,0:T(8,128)(2,1)S(1)} all-to-all(bf16[64,128,128]{2,1,0:T(8,128)(2,1)} %bitcast.213), channel_id=1, replica_groups=mesh['row'=16,'col'=8] {'col'}, dimensions={0} | all-to-all | bytes 4194304 | tf_op jit(solution)/shard_map/all_to_all | solution.py:89
  89.1 2.7 copy.30
  91.8 8.6 %all-to-all-start.1 = ((bf16[1024,8,128]{2,1,0:T(8,128)(2,1)}), bf16[1024,8,128]{2,1,0:T(8,128)(2,1)}, u32[]{:S(2)}, u32[]{:S(2)}) async-start(bf16[1024,8,128]{2,1,0:T(8,128)(2,1)} %copy.30), calls=%async_computation.1 | async-start | bytes 4194304 | tf_op jit(solution)/shard_map/all_to_all | solution.py:90
  101.2 27.3 %all-to-all-done.1 = bf16[1024,8,128]{2,1,0:T(8,128)(2,1)} async-done(((bf16[1024,8,128]{2,1,0:T(8,128)(2,1)}), bf16[1024,8,128]{2,1,0:T(8,128)(2,1)}, u32[]{:S(2)}, u32[]{:S(2)}) %all-to-all-start.1) | async-done | bytes 2097184 | tf_op jit(solution)/shard_map/all_to_all | solution.py:90
  128.5 2.8 exponential_reduce_fusion
  132.2 1.9 fusion.68
  134.1 2.6 copy.35
  136.7 2.3 reshape.76
  139.1 6.3 %all-to-all-start.3 = ((bf16[128,2,2048]{2,1,0:T(2,128)(2,1)}), bf16[128,2,2048]{2,1,0:T(2,128)(2,1)}, u32[]{:S(2)}, u32[]{:S(2)}) async-start(bf16[128,2,2048]{2,1,0:T(2,128)(2,1)} %reshape.76), calls=%async_computation.3 | async-start | bytes 2097152 | tf_op jit(solution)/shard_map/all_to_all | solution.py:102
  146.2 1.7 copy.32
  147.9 2.7 reshape.74
  150.6 12.1 %all-to-all-done.3 = bf16[128,2,2048]{2,1,0:T(2,128)(2,1)} async-done(((bf16[128,2,2048]{2,1,0:T(2,128)(2,1)}), bf16[128,2,2048]{2,1,0:T(2,128)(2,1)}, u32[]{:S(2)}, u32[]{:S(2)}) %all-to-all-start.3) | async-done | bytes 1048608 | tf_op jit(solution)/shard_map/all_to_all | solution.py:102
  162.7 4.6 %all-to-all-start.2 = ((bf16[8,2,32768]{2,1,0:T(2,128)(2,1)}), bf16[8,2,32768]{2,1,0:T(2,128)(2,1)S(1)}, u32[]{:S(2)}, u32[]{:S(2)}) async-start(bf16[8,2,32768]{2,1,0:T(2,128)(2,1)} %reshape.74), calls=%async_computation.2 | async-start | bytes 2097152 | tf_op jit(solution)/shard_map/all_to_all | solution.py:106
  167.3 3.8 reshape.77
  171.5 1.4 copy.66
  172.8 2.7 reshape.78
  175.5 7.5 %all-to-all-done.2 = bf16[8,2,32768]{2,1,0:T(2,128)(2,1)S(1)} async-done(((bf16[8,2,32768]{2,1,0:T(2,128)(2,1)}), bf16[8,2,32768]{2,1,0:T(2,128)(2,1)S(1)}, u32[]{:S(2)}, u32[]{:S(2)}) %all-to-all-start.2) | async-done | bytes 1048608 | tf_op jit(solution)/shard_map/all_to_all | solution.py:106
  183.0 4.2 %all-to-all-start.4 = ((bf16[8,2,32768]{2,1,0:T(2,128)(2,1)}), bf16[8,2,32768]{2,1,0:T(2,128)(2,1)}, u32[]{:S(2)}, u32[]{:S(2)}) async-start(bf16[8,2,32768]{2,1,0:T(2,128)(2,1)} %reshape.78), calls=%async_computation.4 | async-start | bytes 2097152 | tf_op jit(solution)/shard_map/all_to_all | solution.py:107
  187.4 3.1 reshape.75
  190.5 3.1 copy.33
  193.6 1.9 copy.34
  195.5 3.9 fusion.79
  199.4 3.5 all-to-all-done.4
  203.0 3.1 reshape.79
  206.1 1.9 copy.39
  208.0 4.8 %add_convert_fusion = bf16[64,128,128]{2,1,0:T(8,128)(2,1)} fusion(f32[64,128,128]{2,1,0:T(8,128)} %fusion.79, bf16[64,128,64]{1,2,0:T(8,128)(2,1)} %bitcast.225, bf16[128,64]{0,1:T(8,128)(2,1)S(1)} %copy-done), kind=kOutput, calls=%fused_computation.67 | convolution fusion | flops 136314880 | bytes 7356416 | tf_op jit(solution)/shard_map/dot_general | solution.py:117
  212.9 43.0 %while.30 = (s32[]{:T(128)}, f32[128]{0:T(128)S(1)}, f32[128]{0:T(128)S(1)}, f32[128,512]{1,0:T(8,128)S(1)}, f32[128,512]{1,0:T(8,128)S(1)}, /*index=5*/f32[512,...) while((s32[]{:T(128)}, f32[128]{0:T(128)S(1)}, ...), condition=%wide.region_13.14_spmd.clone, body=%wide.region_8.13_spmd.clone.sunk | while | flops 2177501440 | bytes 55328988 | solution.py:137
  216.1 1.3 fusion.159
  217.5 2.1 multiply_convert_fusion.11
  219.6 1.1 convolution_add_fusion.7
  226.8 1.3 fusion.159
  228.2 2.1 multiply_convert_fusion.11
  230.3 1.1 convolution_add_fusion.7
  237.5 1.3 fusion.159
  238.9 2.1 multiply_convert_fusion.11
  241.0 1.1 convolution_add_fusion.7
  248.2 1.3 fusion.159
  249.6 2.1 multiply_convert_fusion.11
  251.7 1.1 convolution_add_fusion.7
  256.8 2.7 fusion.75
  259.6 3.1 copy.40
  262.7 2.8 convolution_add_fusion.4
  265.5 64.7 %all-reduce = (f32[]{:T(128)}, f32[128]{0:T(128)}, f32[128]{0:T(128)}, f32[128,64]{0,1:T(8,128)}) all-reduce(f32[]{:T(128)} %get-tuple-element.229, f32[128]{0:T(128)S(1)} %get-tuple-element.122, f32[128]{0:T(128)S(1)} %get-tuple-element.123, f32[128,64]{0,1:T(8,128)S(1)} %convolution_add_fusion.4), channel_id=1, replica_groups=mesh['row'=16,'col'=8] {'row','col'}, use_global_device_ids=true, to_apply=%region_7.8 | all-reduce | flops 8449 | bytes 67592 | tf_op jit(solution)/shard_map/psum | solution.py:138
  330.8 72.6 %all-reduce.4.cloned.1.call-done = (f32[128,512]{1,0:T(8,128)}, f32[128,512]{1,0:T(8,128)}, f32[512,128]{1,0:T(8,128)}) async-done(((f32[128,512]{1,0:T(8,128)}, f32[128,512]{1,0:T(8,128)}, f32[512,128]{1,0:T(8,128)}), (f32[128,512]{1,0:T(8,128)}, f32[128,512]{1,0:T(8,128)}, f32[512,128]{1,0:T(8,128)})) %all-reduce.4.cloned.1.call-update) | async-done | bytes 786448 | tf_op jit(solution)/shard_map/psum | solution.py:138
  403.3 1.7 copy.95
  405.0 1.7 copy.96
  406.7 1.7 copy.97
  (146 shorter events, 28.3 us)
Async XLA Ops:
  7.2 93.2 %copy-start = (bf16[128,64]{0,1:T(8,128)(2,1)S(1)}, bf16[128,64]{0,1:T(8,128)(2,1)}, u32[]{:S(2)}) copy-start(bf16[128,64]{0,1:T(8,128)(2,1)} %param.19) | copy-start | bytes 49156
  10.2 4.0 copy-start.2
  10.2 4.0 copy-start.12
  10.2 4.0 copy-start.15
  10.2 4.0 copy-start.17
  10.2 4.0 copy-start.22
  21.9 4.0 copy-start.2
  21.9 4.0 copy-start.12
  21.9 4.0 copy-start.15
  21.9 4.0 copy-start.17
  22.0 4.0 copy-start.22
  33.6 4.0 copy-start.2
  33.7 4.0 copy-start.12
  33.7 4.0 copy-start.15
  33.7 4.0 copy-start.17
  33.7 4.0 copy-start.22
  45.4 4.0 copy-start.2
  45.4 4.0 copy-start.12
  45.4 4.0 copy-start.15
  45.4 4.0 copy-start.17
  45.4 4.0 copy-start.22
  91.8 8.6 %copy-start.21 = (s32[8,1024]{1,0:T(8,128)S(1)}, s32[8,1024]{1,0:T(8,128)}, u32[]{:S(2)}) copy-start(s32[8,1024]{1,0:T(8,128)} %param.21) | copy-start | bytes 98308
  91.8 36.7 %all-to-all-start.1 = ((bf16[1024,8,128]{2,1,0:T(8,128)(2,1)}), bf16[1024,8,128]{2,1,0:T(8,128)(2,1)}, u32[]{:S(2)}, u32[]{:S(2)}) async-start(bf16[1024,8,128]{2,1,0:T(8,128)(2,1)} %copy.30), calls=%async_computation.1 | async-start | bytes 4194304 | tf_op jit(solution)/shard_map/all_to_all | solution.py:90
  100.4 28.1 %copy-start.20 = (s32[8,1024]{1,0:T(8,128)S(1)}, s32[8,1024]{1,0:T(8,128)}, u32[]{:S(2)}) copy-start(s32[8,1024]{1,0:T(8,128)} %param.20) | copy-start | bytes 98308
  131.3 1.0 copy-start.9
  139.0 6.3 %copy-start.10 = (bf16[8,1024,64]{1,2,0:T(8,128)(2,1)S(1)}, bf16[8,1024,64]{1,2,0:T(8,128)(2,1)}, u32[]{:S(2)}) copy-start(bf16[8,1024,64]{1,2,0:T(8,128)(2,1)} %copy-done.9) | copy-start | bytes 3145732
  139.1 23.7 %all-to-all-start.3 = ((bf16[128,2,2048]{2,1,0:T(2,128)(2,1)}), bf16[128,2,2048]{2,1,0:T(2,128)(2,1)}, u32[]{:S(2)}, u32[]{:S(2)}) async-start(bf16[128,2,2048]{2,1,0:T(2,128)(2,1)} %reshape.76), calls=%async_computation.3 | async-start | bytes 2097152 | tf_op jit(solution)/shard_map/all_to_all | solution.py:102
  162.7 20.3 %all-to-all-start.2 = ((bf16[8,2,32768]{2,1,0:T(2,128)(2,1)}), bf16[8,2,32768]{2,1,0:T(2,128)(2,1)S(1)}, u32[]{:S(2)}, u32[]{:S(2)}) async-start(bf16[8,2,32768]{2,1,0:T(2,128)(2,1)} %reshape.74), calls=%async_computation.2 | async-start | bytes 2097152 | tf_op jit(solution)/shard_map/all_to_all | solution.py:106
  183.0 4.3 %copy-start.11 = (bf16[8,2,32768]{2,1,0:T(2,128)(2,1)}, bf16[8,2,32768]{2,1,0:T(2,128)(2,1)S(1)}, u32[]{:S(2)}) copy-start(bf16[8,2,32768]{2,1,0:T(2,128)(2,1)S(1)} %all-to-all-done.2) | copy-start | bytes 3145732
  183.0 19.9 %all-to-all-start.4 = ((bf16[8,2,32768]{2,1,0:T(2,128)(2,1)}), bf16[8,2,32768]{2,1,0:T(2,128)(2,1)}, u32[]{:S(2)}, u32[]{:S(2)}) async-start(bf16[8,2,32768]{2,1,0:T(2,128)(2,1)} %reshape.78), calls=%async_computation.4 | async-start | bytes 2097152 | tf_op jit(solution)/shard_map/all_to_all | solution.py:107
  187.3 216.1 %all-reduce.4.cloned.1.call-start = ((), (), s32[]{:S(2)}) async-start(), calls=%async_computation.5 | async-start | bytes 1572864 | tf_op jit(solution)/shard_map/psum | solution.py:138
  206.1 1.9 copy-start.5
  208.0 4.8 %copy-start.3 = (bf16[4,2048,128]{2,1,0:T(8,128)(2,1)S(1)}, bf16[4,2048,128]{2,1,0:T(8,128)(2,1)}, u32[]{:S(2)}) copy-start(bf16[4,2048,128]{2,1,0:T(8,128)(2,1)} %get-tuple-element.458) | copy-start | bytes 6291460
  208.0 4.8 %copy-start.4 = (bf16[128,512]{1,0:T(8,128)(2,1)S(1)}, bf16[128,512]{1,0:T(8,128)(2,1)}, u32[]{:S(2)}) copy-start(bf16[128,512]{1,0:T(8,128)(2,1)} %get-tuple-element.459) | copy-start | bytes 393220
  208.0 4.8 %copy-start.13 = (bf16[128,512]{1,0:T(8,128)(2,1)S(1)}, bf16[128,512]{1,0:T(8,128)(2,1)}, u32[]{:S(2)}) copy-start(bf16[128,512]{1,0:T(8,128)(2,1)} %get-tuple-element.472) | copy-start | bytes 393220
  208.0 4.8 %copy-start.16 = (f32[128]{0:T(128)S(1)}, f32[128]{0:T(128)}, u32[]{:S(2)}) copy-start(f32[128]{0:T(128)} %get-tuple-element.473) | copy-start | bytes 1540
  208.0 4.8 %copy-start.18 = (f32[128]{0:T(128)S(1)}, f32[128]{0:T(128)}, u32[]{:S(2)}) copy-start(f32[128]{0:T(128)} %get-tuple-element.474) | copy-start | bytes 1540
  208.0 4.8 %copy-start.23 = (bf16[512,128]{1,0:T(8,128)(2,1)S(1)}, bf16[512,128]{1,0:T(8,128)(2,1)}, u32[]{:S(2)}) copy-start(bf16[512,128]{1,0:T(8,128)(2,1)} %get-tuple-element.480) | copy-start | bytes 393220
  214.5 1.6 copy-start.14
  225.2 1.6 copy-start.14
  235.9 1.6 copy-start.14
  246.6 1.6 copy-start.14
  255.9 0.7 copy-start.7
  255.9 0.8 copy-start.8
  255.9 0.9 copy-start.19
  255.9 3.6 copy-start.6
  262.7 145.7 %copy-start.1 = (bf16[128,64]{0,1:T(8,128)(2,1)S(1)}, bf16[128,64]{0,1:T(8,128)(2,1)}, u32[]{:S(2)}) copy-start(bf16[128,64]{0,1:T(8,128)(2,1)} %param.19) | copy-start | bytes 49156
Sparse Core Ops, SparseCore 0:
  256.9 146.3 all-reduce.3
where the time goes:
time: 418 us; the launch traced here: 416 us
  waiting for transfers between devices  123 us (29%)
  blocking collectives  99.5 us (24%)
  matrix products  88.2 us (21%)
  local copies, waits for them, and re-layouts  46 us (11%)
  starting transfers between devices  23.7 us (6%)
  other arithmetic  18.7 us (4%)
  between operations  16.2 us (4%)
    psum x1, waiting for transfers between devices, shards(): lax.psum((loss_part, totals[0], totals[1], totals[2], totals[3], totals[4...  72.6 us
    psum x1, blocking collectives, shards(): lax.psum((loss_part, totals[0], totals[1], totals[2], totals[3], totals[4...  64.7 us
    all_to_all x1, blocking collectives, shards(): lax.all_to_all(pair_out, 'col', split_axis=0, concat_axis=1, tiled=True)  34.8 us
    all_to_all x1, waiting for transfers between devices, shards(): lax.all_to_all(jnp.swapaxes(rows_pair, 0, 1), ('row', 'col'), split_axis=...  27.3 us
    unnamed x45, local copies, waits for them, and re-layouts  23.8 us
    dot_general x14, matrix products, inner(): lax.dot_general(left, right, (((0,), (0,)), ((), ())), preferred_element_...  19.9 us
    dot_general x4, matrix products, advance(): update = jnp.dot(hidden, out_weight, preferred_element_type=jnp.float32)  18.9 us
    dot_general x4, matrix products, advance(): gate_pre = jnp.dot(normed, gate_weight, preferred_element_type=jnp.float32)  15.9 us
  transfers between devices with their start and end apart: 5, of which 5 were waited for; matrix products, arithmetic and copies ran while one was open for 8% of the time, Pallas kernels for 0%

commit v1 on v0

--- a/solution.py
+++ b/solution.py
@@ -135,10 +135,10 @@
         )
 
     totals, unused = lax.scan(backward_one, start, (blocks, grad_blocks))
-    summed = lax.psum(
-        (loss_part, totals[0], totals[1], totals[2], totals[3], totals[4], grad_head),
-        ("row", "col"),
+    one_axis = lax.psum(
+        (loss_part, totals[0], totals[1], totals[2], totals[3], totals[4], grad_head), "col"
     )
+    summed = lax.psum(one_axis, "row")
     loss = summed[0] / (tokens * tokens)
     return (pair_out, loss, summed[1], summed[2], summed[3], summed[4], summed[5], summed[6])
 

time: 418 us -> 477 us (1.14)
  blocking collectives: 99.5 us -> 130 us
  waiting for transfers between devices: 123 us -> 151 us
    psum x0 -> x1, blocking collectives: none -> 62.4 us  [shards(): summed = lax.psum(one_axis, 'row')]
    psum x1, blocking collectives: 64.7 us -> 32.5 us  [shards(): lax.psum((loss_part, totals[0], totals[1], totals[2], totals[3], totals[4...]
    psum x0 -> x1, waiting for transfers between devices: none -> 19.1 us  [shards(): summed = lax.psum(one_axis, 'row')]
    psum x1, waiting for transfers between devices: 72.6 us -> 80 us  [shards(): lax.psum((loss_part, totals[0], totals[1], totals[2], totals[3], totals[4...]
    unnamed x45 -> x47, local copies, waits for them, and re-layouts: 23.8 us -> 23.8 us
  transfers between devices with their start and end apart: 5 -> 6, of which waited for: 5 -> 6; matrix products, arithmetic and copies ran while one was open for 8% -> 8% of each run, Pallas kernels for 0% -> 0%
where the time goes in v1:
time: 477 us; the launch traced here: 475 us
  waiting for transfers between devices  151 us (32%)
  blocking collectives  130 us (27%)
  matrix products  87.7 us (18%)
  local copies, waits for them, and re-layouts  46.7 us (10%)
  starting transfers between devices  24 us (5%)
  other arithmetic  19.7 us (4%)
  between operations  16.2 us (3%)
    psum x1, waiting for transfers between devices, shards(): lax.psum((loss_part, totals[0], totals[1], totals[2], totals[3], totals[4...  80 us
    psum x1, blocking collectives, shards(): summed = lax.psum(one_axis, 'row')  62.4 us
    all_to_all x1, blocking collectives, shards(): lax.all_to_all(pair_out, 'col', split_axis=0, concat_axis=1, tiled=True)  34.8 us
    psum x1, blocking collectives, shards(): lax.psum((loss_part, totals[0], totals[1], totals[2], totals[3], totals[4...  32.5 us
    all_to_all x1, waiting for transfers between devices, shards(): lax.all_to_all(jnp.swapaxes(rows_pair, 0, 1), ('row', 'col'), split_axis=...  27.3 us
    unnamed x47, local copies, waits for them, and re-layouts  23.8 us
    dot_general x14, matrix products, inner(): lax.dot_general(left, right, (((0,), (0,)), ((), ())), preferred_element_...  19.3 us
    psum x1, waiting for transfers between devices, shards(): summed = lax.psum(one_axis, 'row')  19.1 us
  transfers between devices with their start and end apart: 6, of which 6 were waited for; matrix products, arithmetic and copies ran while one was open for 8% of the time, Pallas kernels for 0%

profile of v1, /device:TPU:1, one launch (start us, length us, event | category | flops | bytes accessed | tf_op | source)
XLA Modules:
  0.0 475.4 jit_solution(1439036759768985952)
XLA Ops:
  7.2 47.0 %while.29 = (s32[]{:T(128)}, bf16[4,2048,128]{2,1,0:T(8,128)(2,1)}, bf16[4,2048,128]{2,1,0:T(8,128)(2,1)}, f32[128]{0:T(128)}, f32[128]{0:T(128)}, /*index=5*/bf...) while((s32[]{:T(128)}, bf16[4,2048,128]{2,1,0:T(8,128)(2,1)}, ...), condition=%wide.region_3.4_spmd, body=%wide.region_0.3_spmd.sunk | while | flops 817104896 | bytes 21462268 | solution.py:88
  7.2 1.3 convert_reduce_fusion.4
  8.5 1.7 fusion.136
  10.2 4.0 fusion.137
  14.2 4.7 fusion.138
  18.9 1.2 convert_reduce_fusion.4
  20.2 1.7 fusion.136
  22.0 4.0 fusion.137
  26.0 4.7 fusion.138
  30.7 1.2 convert_reduce_fusion.4
  32.0 1.7 fusion.136
  33.7 4.0 fusion.137
  37.7 4.7 fusion.138
  42.4 1.2 convert_reduce_fusion.4
  43.7 1.7 fusion.136
  45.5 4.0 fusion.137
  49.5 4.7 fusion.138
  54.2 34.8 %all_to_all.90 = bf16[64,128,128]{2,1,0:T(8,128)(2,1)S(1)} all-to-all(bf16[64,128,128]{2,1,0:T(8,128)(2,1)} %bitcast.213), channel_id=1, replica_groups=mesh['row'=16,'col'=8] {'col'}, dimensions={0} | all-to-all | bytes 4194304 | tf_op jit(solution)/shard_map/all_to_all | solution.py:89
  89.1 2.7 copy.30
  91.8 8.6 %all-to-all-start.1 = ((bf16[1024,8,128]{2,1,0:T(8,128)(2,1)}), bf16[1024,8,128]{2,1,0:T(8,128)(2,1)}, u32[]{:S(2)}, u32[]{:S(2)}) async-start(bf16[1024,8,128]{2,1,0:T(8,128)(2,1)} %copy.30), calls=%async_computation.1 | async-start | bytes 4194304 | tf_op jit(solution)/shard_map/all_to_all | solution.py:90
  101.3 27.3 %all-to-all-done.1 = bf16[1024,8,128]{2,1,0:T(8,128)(2,1)} async-done(((bf16[1024,8,128]{2,1,0:T(8,128)(2,1)}), bf16[1024,8,128]{2,1,0:T(8,128)(2,1)}, u32[]{:S(2)}, u32[]{:S(2)}) %all-to-all-start.1) | async-done | bytes 2097184 | tf_op jit(solution)/shard_map/all_to_all | solution.py:90
  128.6 2.8 exponential_reduce_fusion
  132.3 1.9 fusion.68
  134.1 2.6 copy.35
  136.8 2.3 reshape.76
  139.1 6.3 %all-to-all-start.3 = ((bf16[128,2,2048]{2,1,0:T(2,128)(2,1)}), bf16[128,2,2048]{2,1,0:T(2,128)(2,1)}, u32[]{:S(2)}, u32[]{:S(2)}) async-start(bf16[128,2,2048]{2,1,0:T(2,128)(2,1)} %reshape.76), calls=%async_computation.3 | async-start | bytes 2097152 | tf_op jit(solution)/shard_map/all_to_all | solution.py:102
  145.4 1.8 multiply_convert_fusion.7
  147.2 2.6 copy.32
  149.9 2.7 reshape.74
  152.5 10.2 %all-to-all-done.3 = bf16[128,2,2048]{2,1,0:T(2,128)(2,1)} async-done(((bf16[128,2,2048]{2,1,0:T(2,128)(2,1)}), bf16[128,2,2048]{2,1,0:T(2,128)(2,1)}, u32[]{:S(2)}, u32[]{:S(2)}) %all-to-all-start.3) | async-done | bytes 1048608 | tf_op jit(solution)/shard_map/all_to_all | solution.py:102
  162.8 4.6 all-to-all-start.2
  167.3 3.8 reshape.77
  171.5 1.4 copy.66
  172.9 2.7 reshape.78
  175.5 7.5 %all-to-all-done.2 = bf16[8,2,32768]{2,1,0:T(2,128)(2,1)S(1)} async-done(((bf16[8,2,32768]{2,1,0:T(2,128)(2,1)}), bf16[8,2,32768]{2,1,0:T(2,128)(2,1)S(1)}, u32[]{:S(2)}, u32[]{:S(2)}) %all-to-all-start.2) | async-done | bytes 1048608 | tf_op jit(solution)/shard_map/all_to_all | solution.py:106
  183.1 4.2 all-to-all-start.4
  187.4 3.1 reshape.75
  190.5 1.9 copy.34
  192.5 3.9 fusion.79
  196.4 6.6 %all-to-all-done.4 = bf16[8,2,32768]{2,1,0:T(2,128)(2,1)} async-done(((bf16[8,2,32768]{2,1,0:T(2,128)(2,1)}), bf16[8,2,32768]{2,1,0:T(2,128)(2,1)}, u32[]{:S(2)}, u32[]{:S(2)}) %all-to-all-start.4) | async-done | bytes 1048608 | tf_op jit(solution)/shard_map/all_to_all | solution.py:107
  203.0 3.1 reshape.79
  206.1 1.9 copy.39
  208.1 4.8 %add_convert_fusion = bf16[64,128,128]{2,1,0:T(8,128)(2,1)} fusion(f32[64,128,128]{2,1,0:T(8,128)} %fusion.79, bf16[64,128,64]{1,2,0:T(8,128)(2,1)} %bitcast.223, bf16[128,64]{0,1:T(8,128)(2,1)S(1)} %copy-done), kind=kOutput, calls=%fused_computation.67 | convolution fusion | flops 136314880 | bytes 7356416 | tf_op jit(solution)/shard_map/dot_general | solution.py:117
  212.9 42.8 %while.30 = (s32[]{:T(128)}, f32[128]{0:T(128)S(1)}, f32[128]{0:T(128)S(1)}, f32[128,512]{1,0:T(8,128)S(1)}, f32[128,512]{1,0:T(8,128)S(1)}, /*index=5*/f32[512,...) while((s32[]{:T(128)}, f32[128]{0:T(128)S(1)}, ...), condition=%wide.region_14.15_spmd.clone, body=%wide.region_9.14_spmd.clone.sunk | while | flops 2177501440 | bytes 55328988 | solution.py:137
  216.2 1.3 fusion.159
  217.5 2.1 multiply_convert_fusion.11
  226.9 1.3 fusion.159
  228.2 2.1 multiply_convert_fusion.11
  230.4 1.1 convolution_add_fusion.7
  237.6 1.3 fusion.159
  238.9 2.1 multiply_convert_fusion.11
  248.3 1.3 fusion.159
  249.6 2.1 multiply_convert_fusion.11
  256.9 80.0 %all-reduce.9.cloned.1.call-done = (f32[128,512]{1,0:T(8,128)}, f32[128,512]{1,0:T(8,128)}, f32[512,128]{1,0:T(8,128)}) async-done(((f32[128,512]{1,0:T(8,128)}, f32[128,512]{1,0:T(8,128)}, f32[512,128]{1,0:T(8,128)}), (f32[128,512]{1,0:T(8,128)}, f32[128,512]{1,0:T(8,128)}, f32[512,128]{1,0:T(8,128)})) %all-reduce.9.cloned.1.call-update) | async-done | bytes 786448 | tf_op jit(solution)/shard_map/psum | solution.py:138
  336.9 3.5 copy.33
  340.5 2.5 fusion.75
  343.0 2.4 copy.40
  345.4 2.4 convolution_add_fusion.4
  347.8 32.5 %all-reduce.2 = (f32[]{:T(128)}, f32[128]{0:T(128)S(1)}, f32[128]{0:T(128)S(1)}, f32[128,64]{0,1:T(8,128)S(1)}) all-reduce(f32[]{:T(128)} %get-tuple-element.236, f32[128]{0:T(128)S(1)} %get-tuple-element.122, f32[128]{0:T(128)S(1)} %get-tuple-element.123, ...), channel_id=1, replica_groups=mesh['row'=16,'col'=8] {'col'}, use_global_device_ids=true, to_apply=%region_7.8 | all-reduce | flops 8449 | bytes 67592 | tf_op jit(solution)/shard_map/psum | solution.py:138
  380.3 62.4 %all-reduce = (f32[]{:T(128)}, f32[128]{0:T(128)}, f32[128]{0:T(128)}, f32[128,64]{0,1:T(8,128)}) all-reduce(f32[]{:T(128)} %get-tuple-element.222, f32[128]{0:T(128)S(1)} %get-tuple-element.223, f32[128]{0:T(128)S(1)} %get-tuple-element.224, f32[128,64]{0,1:T(8,128)S(1)} %get-tuple-element.225), channel_id=1, replica_groups=mesh['row'=16,'col'=8] {'row'}, use_global_device_ids=true, to_apply=%region_8.9 | all-reduce | flops 8449 | bytes 67592 | tf_op jit(solution)/shard_map/psum | solution.py:141
  443.3 19.1 %all-reduce.7.cloned.1.call-done = (f32[128,512]{1,0:T(8,128)}, f32[128,512]{1,0:T(8,128)}, f32[512,128]{1,0:T(8,128)}) async-done(((f32[128,512]{1,0:T(8,128)}, f32[128,512]{1,0:T(8,128)}, f32[512,128]{1,0:T(8,128)}), (f32[128,512]{1,0:T(8,128)}, f32[128,512]{1,0:T(8,128)}, f32[512,128]{1,0:T(8,128)})) %all-reduce.7.cloned.1.call-update) | async-done | bytes 786448 | tf_op jit(solution)/shard_map/psum | solution.py:141
  462.5 1.7 copy.98
  464.1 1.7 copy.99
  465.8 1.7 copy.100
  (152 shorter events, 31.1 us)
Async XLA Ops:
  7.2 93.3 %copy-start = (bf16[128,64]{0,1:T(8,128)(2,1)S(1)}, bf16[128,64]{0,1:T(8,128)(2,1)}, u32[]{:S(2)}) copy-start(bf16[128,64]{0,1:T(8,128)(2,1)} %param.19) | copy-start | bytes 49156
  10.2 4.0 copy-start.2
  10.2 4.0 copy-start.13
  10.2 4.0 copy-start.16
  10.2 4.0 copy-start.18
  10.2 4.0 copy-start.23
  21.9 4.0 copy-start.2
  21.9 4.0 copy-start.13
  21.9 4.0 copy-start.16
  21.9 4.0 copy-start.18
  22.0 4.0 copy-start.23
  33.7 4.0 copy-start.2
  33.7 4.0 copy-start.13
  33.7 4.0 copy-start.16
  33.7 4.0 copy-start.18
  33.7 4.0 copy-start.23
  45.4 4.0 copy-start.2
  45.4 4.0 copy-start.13
  45.4 4.0 copy-start.16
  45.4 4.0 copy-start.18
  45.4 4.0 copy-start.23
  91.8 8.6 %copy-start.22 = (s32[8,1024]{1,0:T(8,128)S(1)}, s32[8,1024]{1,0:T(8,128)}, u32[]{:S(2)}) copy-start(s32[8,1024]{1,0:T(8,128)} %param.21) | copy-start | bytes 98308
  91.8 36.7 %all-to-all-start.1 = ((bf16[1024,8,128]{2,1,0:T(8,128)(2,1)}), bf16[1024,8,128]{2,1,0:T(8,128)(2,1)}, u32[]{:S(2)}, u32[]{:S(2)}) async-start(bf16[1024,8,128]{2,1,0:T(8,128)(2,1)} %copy.30), calls=%async_computation.1 | async-start | bytes 4194304 | tf_op jit(solution)/shard_map/all_to_all | solution.py:90
  100.4 28.1 %copy-start.21 = (s32[8,1024]{1,0:T(8,128)S(1)}, s32[8,1024]{1,0:T(8,128)}, u32[]{:S(2)}) copy-start(s32[8,1024]{1,0:T(8,128)} %param.20) | copy-start | bytes 98308
  131.3 1.0 copy-start.10
  139.1 6.3 %copy-start.11 = (bf16[8,1024,64]{1,2,0:T(8,128)(2,1)S(1)}, bf16[8,1024,64]{1,2,0:T(8,128)(2,1)}, u32[]{:S(2)}) copy-start(bf16[8,1024,64]{1,2,0:T(8,128)(2,1)} %copy-done.10) | copy-start | bytes 3145732
  139.1 23.7 %all-to-all-start.3 = ((bf16[128,2,2048]{2,1,0:T(2,128)(2,1)}), bf16[128,2,2048]{2,1,0:T(2,128)(2,1)}, u32[]{:S(2)}, u32[]{:S(2)}) async-start(bf16[128,2,2048]{2,1,0:T(2,128)(2,1)} %reshape.76), calls=%async_computation.3 | async-start | bytes 2097152 | tf_op jit(solution)/shard_map/all_to_all | solution.py:102
  162.8 20.3 %all-to-all-start.2 = ((bf16[8,2,32768]{2,1,0:T(2,128)(2,1)}), bf16[8,2,32768]{2,1,0:T(2,128)(2,1)S(1)}, u32[]{:S(2)}, u32[]{:S(2)}) async-start(bf16[8,2,32768]{2,1,0:T(2,128)(2,1)} %reshape.74), calls=%async_computation.2 | async-start | bytes 2097152 | tf_op jit(solution)/shard_map/all_to_all | solution.py:106
  183.1 4.3 copy-start.12
  183.1 19.9 %all-to-all-start.4 = ((bf16[8,2,32768]{2,1,0:T(2,128)(2,1)}), bf16[8,2,32768]{2,1,0:T(2,128)(2,1)}, u32[]{:S(2)}, u32[]{:S(2)}) async-start(bf16[8,2,32768]{2,1,0:T(2,128)(2,1)} %reshape.78), calls=%async_computation.4 | async-start | bytes 2097152 | tf_op jit(solution)/shard_map/all_to_all | solution.py:107
  187.3 149.6 %all-reduce.9.cloned.1.call-start = ((), (), s32[]{:S(2)}) async-start(), calls=%async_computation.6 | async-start | bytes 1572864 | tf_op jit(solution)/shard_map/psum | solution.py:138
  190.5 5.9 %copy-start.5 = (bf16[1024,8,64]{2,1,0:T(8,128)(2,1)}, bf16[1024,8,64]{2,1,0:T(8,128)(2,1)S(1)}, u32[]{:S(2)}) copy-start(bf16[1024,8,64]{2,1,0:T(8,128)(2,1)S(1)} %reshape.75) | copy-start | bytes 3145732
  206.1 1.9 copy-start.6
  208.0 4.9 %copy-start.3 = (bf16[4,2048,128]{2,1,0:T(8,128)(2,1)S(1)}, bf16[4,2048,128]{2,1,0:T(8,128)(2,1)}, u32[]{:S(2)}) copy-start(bf16[4,2048,128]{2,1,0:T(8,128)(2,1)} %get-tuple-element.471) | copy-start | bytes 6291460
  208.0 4.9 %copy-start.4 = (bf16[128,512]{1,0:T(8,128)(2,1)S(1)}, bf16[128,512]{1,0:T(8,128)(2,1)}, u32[]{:S(2)}) copy-start(bf16[128,512]{1,0:T(8,128)(2,1)} %get-tuple-element.472) | copy-start | bytes 393220
  208.0 4.9 %copy-start.14 = (bf16[128,512]{1,0:T(8,128)(2,1)S(1)}, bf16[128,512]{1,0:T(8,128)(2,1)}, u32[]{:S(2)}) copy-start(bf16[128,512]{1,0:T(8,128)(2,1)} %get-tuple-element.485) | copy-start | bytes 393220
  208.0 4.8 %copy-start.17 = (f32[128]{0:T(128)S(1)}, f32[128]{0:T(128)}, u32[]{:S(2)}) copy-start(f32[128]{0:T(128)} %get-tuple-element.486) | copy-start | bytes 1540
  208.0 4.8 %copy-start.19 = (f32[128]{0:T(128)S(1)}, f32[128]{0:T(128)}, u32[]{:S(2)}) copy-start(f32[128]{0:T(128)} %get-tuple-element.487) | copy-start | bytes 1540
  208.0 4.8 %copy-start.24 = (bf16[512,128]{1,0:T(8,128)(2,1)S(1)}, bf16[512,128]{1,0:T(8,128)(2,1)}, u32[]{:S(2)}) copy-start(bf16[512,128]{1,0:T(8,128)(2,1)} %get-tuple-element.501) | copy-start | bytes 393220
  214.6 1.6 copy-start.15
  225.3 1.6 copy-start.15
  236.0 1.6 copy-start.15
  246.7 1.6 copy-start.15
  255.7 0.7 copy-start.8
  255.7 0.8 copy-start.9
  255.7 0.9 copy-start.20
  256.6 205.8 %all-reduce.7.cloned.1.call-start = ((), (), s32[]{:S(2)}) async-start(), calls=%async_computation.5 | async-start | bytes 1572864 | tf_op jit(solution)/shard_map/psum | solution.py:141
  340.5 2.5 copy-start.7
  345.4 122.1 %copy-start.1 = (bf16[128,64]{0,1:T(8,128)(2,1)S(1)}, bf16[128,64]{0,1:T(8,128)(2,1)}, u32[]{:S(2)}) copy-start(bf16[128,64]{0,1:T(8,128)(2,1)} %param.19) | copy-start | bytes 49156
Sparse Core Ops, SparseCore 0:
  256.7 80.1 all-reduce.8
  339.6 122.8 all-reduce.6
